TPU v7x, 128 devices: a whole 4x4x4 slice. The times are simulated.
128 devices in a mesh: mem: 4 (over x), space: 32 (over y, z, core).
Axes of the slice: x: 4, y: 4, z: 4, core: 2. Of those that a mesh axis runs over, the one named last changes fastest.
Arguments:
- log_perm: float32 [8, 128, 128, 128], P('mem', 'space'), may hold values from -4 to 4
- saturation: float32 [128, 128, 128], P('space'), may hold values from 0.1 to 0.9
- pressure_init: float32 [128, 128, 128], P('space'), may hold values from -3 to 3
- wells: int32 [64], replicated, may hold values from 0 to 2097151
- well_rate: float32 [64], replicated, may hold values from -4 to 4
- obs_index: int32 [512, 8], replicated, may hold values from 0 to 2097151, as said below
- obs_weight: float32 [512, 8], replicated, may hold values from -2 to 2
- obs_value: float32 [512], replicated, may hold values from -5 to 5
- obs_var: float32 [512], replicated, may hold values from 0.1 to 1
- noise: float32 [8, 512], replicated, may hold values from -5 to 5
Outputs:
- updated_perm: float32 [8, 128, 128, 128], P(None, 'space', 'mem')
Inputs may be any that keep to these rules, and one draw needn't show every extreme that they name: `obs_index`: observation o reads only cells of the grid row o % 128 along the first dimension.
All inputs are finite; a program needn't handle non-finite values.
Results may differ from a plain program's by a relative error of at most 0.00007.
Values sent between devices are 32-bit elements; how exact they have to be, the bound alone decides.
No kernel may reach another device: no remote copies, remote signals or barrier semaphores. Data moves between devices by JAX's collectives and lax.ppermute only.
A program may use at most 128 MiB of HBM per device.

v0:
```python
import jax
import jax.numpy as jnp
from jax import lax
from jax.sharding import PartitionSpec as P

SWEEPS = 6
water_visc = 1.0
oil_visc = 4.0
time_step = 0.1
storage = 1.0
inflation = 4.0


def padded(cells, sides, width):
    for axis, dim in sides:
        count = lax.axis_size(axis)
        ends = count - 1
        head = lax.slice_in_dim(cells, 0, width, axis=dim)
        tail = lax.slice_in_dim(cells, cells.shape[dim] - width, cells.shape[dim], axis=dim)
        cells = jnp.concatenate(
            [
                lax.ppermute(tail, axis, [(i, (i + 1) % count) for i in range(ends)]),
                cells,
                lax.ppermute(head, axis, [((i + 1) % count, i) for i in range(ends)]),
            ],
            axis=dim,
        )
    return cells


def pad_plane(field):
    return jnp.pad(field, ((0, 0), (0, 0), (1, 1), (1, 1)))


def beside_all(field):
    return [
        field[:, 2:, 1:-1, 1:-1],
        field[:, :-2, 1:-1, 1:-1],
        field[:, 1:-1, 2:, 1:-1],
        field[:, 1:-1, :-2, 1:-1],
        field[:, 1:-1, 1:-1, 2:],
        field[:, 1:-1, 1:-1, :-2],
    ]


def middle(field):
    return field[:, 1:-1, 1:-1, 1:-1]


def props(perm, sat):
    water = sat * sat / water_visc
    oil = (1.0 - sat) * (1.0 - sat) / oil_visc
    total = water + oil
    return (perm * total, water / total)


def saturate(perm_pad, sat_pad, press_pad, source):
    lam, frac = props(perm_pad, sat_pad)
    lam_mid, frac_mid, press_mid = (middle(lam), middle(frac), middle(press_pad))
    outflow = jnp.zeros_like(lam_mid)
    for lam_next, frac_next, press_next in zip(
        beside_all(lam), beside_all(frac), beside_all(press_pad)
    ):
        flux = 0.5 * (lam_mid + lam_next) * (press_mid - press_next)
        outflow = outflow + jnp.maximum(flux, 0.0) * frac_mid + jnp.minimum(flux, 0.0) * frac_next
    water = jnp.maximum(source, 0.0) + jnp.minimum(source, 0.0) * frac_mid
    return jnp.clip(middle(sat_pad) + time_step * (water - outflow), 0.0, 1.0)


def pressure(perm_pad, sat_pad, press_pad, source):
    lam, frac = props(perm_pad, sat_pad)
    lam_mid = middle(lam)
    numer = storage * middle(press_pad) + source
    denom = storage + jnp.zeros_like(lam_mid)
    for lam_next, press_next in zip(beside_all(lam), beside_all(press_pad)):
        trans = 0.5 * (lam_mid + lam_next)
        numer = numer + trans * press_next
        denom = denom + trans
    return numer / denom


def sources(wells, well_rate, first_row, rows, ny, nz):
    plane = ny * nz
    well_x = wells // plane
    rest = wells - well_x * plane
    local_x = well_x - first_row
    valid = (local_x >= 0) & (local_x < rows)
    target = jnp.where(valid, local_x * plane + rest, 0)
    field = jnp.zeros((rows * plane,), jnp.float32).at[target].add(jnp.where(valid, well_rate, 0.0))
    return field.reshape(rows, ny, nz)


def body(
    log_perm,
    saturation,
    pressure_init,
    wells,
    well_rate,
    obs_index,
    obs_weight,
    obs_value,
    obs_var,
    noise,
):
    members, width, ny, nz = log_perm.shape
    shape = (members, width, ny, nz)
    perm = jnp.exp(log_perm)
    sat = jnp.broadcast_to(saturation, shape)
    press = jnp.broadcast_to(pressure_init, shape)
    place = lax.axis_index("space")
    source = sources(wells, well_rate, place * width, width, ny, nz)
    stacked = padded(jnp.stack([perm, sat, press]), (("space", 2),), 1)
    perm_pad = pad_plane(stacked[0])
    sat_ext = stacked[1]
    press_ext = stacked[2]
    for sweep in range(SWEEPS):
        sat = saturate(perm_pad, pad_plane(sat_ext), pad_plane(press_ext), source)
        sat_ext = padded(sat, (("space", 1),), 1)
        press = pressure(perm_pad, pad_plane(sat_ext), pad_plane(press_ext), source)
        if sweep + 1 < SWEEPS:
            press_ext = padded(press, (("space", 1),), 1)
    cells = width * ny * nz
    flat = press.reshape(members, cells)
    local = obs_index - place * cells
    valid = (local >= 0) & (local < cells)
    picked = jnp.take(flat, jnp.where(valid, local, 0), axis=1)
    partial_value = jnp.sum(picked * jnp.where(valid, obs_weight, 0.0)[None], axis=2)
    summed = lax.psum(partial_value, "space")
    predicted = lax.all_gather(summed, "mem", axis=0, tiled=True)
    ensemble = predicted.shape[0]
    high = lax.Precision.HIGHEST
    dev = predicted - jnp.mean(predicted, axis=0, keepdims=True)
    cov = jnp.dot(dev.T, dev, precision=high) / (ensemble - 1) + inflation * jnp.diag(obs_var)
    resid = obs_value[None, :] + jnp.sqrt(inflation * obs_var)[None, :] * noise - predicted
    factor = jnp.linalg.cholesky(cov)
    half = lax.linalg.triangular_solve(factor, resid.T, left_side=True, lower=True)
    solved = lax.linalg.triangular_solve(factor, half, left_side=True, lower=True, transpose_a=True)
    weights = jnp.dot(dev, solved, precision=high) / (ensemble - 1)
    mixing = (
        jnp.eye(ensemble, dtype=jnp.float32) + weights - jnp.mean(weights, axis=0, keepdims=True)
    )
    columns = lax.all_to_all(log_perm, "mem", split_axis=2, concat_axis=0, tiled=True)
    return jnp.tensordot(mixing.T, columns, axes=1, precision=high)


def solution(mesh):
    placed = (
        P("mem", "space", None, None),
        P("space", None, None),
        P("space", None, None),
        P(),
        P(),
        P(),
        P(),
        P(),
        P(),
        P(),
    )
    return jax.shard_map(
        body, mesh=mesh, in_specs=placed, out_specs=P(None, "space", "mem", None), check_vma=False
    )
```

profile of v0, /device:TPU:0, one launch (start us, length us, event | category | flops | bytes accessed | tf_op | source)
XLA Modules:
  0.0 506.8 jit_solution(8930795188840093129)
XLA Ops:
  6.8 3.5 collective-permute-done.1
  12.8 2.6 fusion.189
  15.4 7.9 %collective-permute-start.2 = (f32[2,1,128,128]{3,2,1,0:T(8,128)S(1)}, f32[2,1,128,128]{3,2,1,0:T(8,128)S(1)}, u32[]{:S(2)}, u32[]{:S(2)}) collective-permute-start(f32[2,1,128,128]{3,2,1,0:T(8,128)S(1)} %get-tuple-element.64), channel_id=1, source_target_pairs={{0,1},{1,2},{2,3},{3,4},{4,5},{5,6},{6,7},{7,8},{8,9},{9,10},{10,1... | collective-permute-start | bytes 393224 | tf_op jit(solution)/shard_map/ppermute | solution.py:22
  24.6 1.9 collective-permute-done.3
  29.9 5.9 %collective-permute-start.5 = (f32[2,1,128,128]{3,2,1,0:T(8,128)S(1)}, f32[2,1,128,128]{3,2,1,0:T(8,128)S(1)}, u32[]{:S(2)}, u32[]{:S(2)}) collective-permute-start(f32[2,1,128,128]{3,2,1,0:T(8,128)S(1)} %get-tuple-element.63), channel_id=1, source_target_pairs={{0,1},{1,2},{2,3},{3,4},{4,5},{5,6},{6,7},{7,8},{8,9},{9,10},{10,1... | collective-permute-start | bytes 393224 | tf_op jit(solution)/shard_map/ppermute | solution.py:22
  37.3 2.7 fusion.155
  40.0 4.6 collective-permute-start.6
  46.0 3.9 collective-permute-done.7
  53.5 6.3 %collective-permute-start.9 = (f32[2,1,128,128]{3,2,1,0:T(8,128)S(1)}, f32[2,1,128,128]{3,2,1,0:T(8,128)S(1)}, u32[]{:S(2)}, u32[]{:S(2)}) collective-permute-start(f32[2,1,128,128]{3,2,1,0:T(8,128)S(1)} %get-tuple-element.59), channel_id=1, source_target_pairs={{0,1},{1,2},{2,3},{3,4},{4,5},{5,6},{6,7},{7,8},{8,9},{9,10},{10,1... | collective-permute-start | bytes 393224 | tf_op jit(solution)/shard_map/ppermute | solution.py:22
  61.0 2.6 fusion.121
  63.7 4.6 collective-permute-start.10
  69.6 3.9 collective-permute-done.11
  77.1 6.1 %collective-permute-start.13 = (f32[2,1,128,128]{3,2,1,0:T(8,128)S(1)}, f32[2,1,128,128]{3,2,1,0:T(8,128)S(1)}, u32[]{:S(2)}, u32[]{:S(2)}) collective-permute-start(f32[2,1,128,128]{3,2,1,0:T(8,128)S(1)} %get-tuple-element.55), channel_id=1, source_target_pairs={{0,1},{1,2},{2,3},{3,4},{4,5},{5,6},{6,7},{7,8},{8,9},{9,10},{10,1... | collective-permute-start | bytes 393224 | tf_op jit(solution)/shard_map/ppermute | solution.py:22
  84.7 2.6 fusion.87
  88.1 4.6 collective-permute-start.14
  95.2 4.3 all-to-all-start
  100.1 3.3 multiply_divide_fusion.1
  103.5 1.4 fusion.103
  107.7 5.5 %collective-permute-start.17 = (f32[2,1,128,128]{3,2,1,0:T(8,128)}, f32[2,1,128,128]{3,2,1,0:T(8,128)S(1)}, u32[]{:S(2)}, u32[]{:S(2)}) collective-permute-start(f32[2,1,128,128]{3,2,1,0:T(8,128)} %get-tuple-element.51), channel_id=1, source_target_pairs={{0,1},{1,2},{2,3},{3,4},{4,5},{5,6},{6,7},{7,8},{8,9},{9,10},{10,1... | collective-permute-start | bytes 393224 | tf_op jit(solution)/shard_map/ppermute | solution.py:22
  115.8 1.7 select_maximum_fusion.6
  117.5 3.7 fusion.53
  121.2 4.0 collective-permute-start.18
  125.2 1.7 collective-permute-start.19
  127.0 6.7 %collective-permute-done.19 = f32[2,1,128,128]{3,2,1,0:T(8,128)S(1)} collective-permute-done((f32[2,1,128,128]{3,2,1,0:T(8,128)S(1)}, f32[2,1,128,128]{3,2,1,0:T(8,128)S(1)}, u32[]{:S(2)}, u32[]{:S(2)}) %collective-permute-start.19) | collective-permute-done | bytes 131104 | tf_op jit(solution)/shard_map/ppermute | solution.py:24
  137.2 7.6 %collective-permute-start.21 = (f32[2,1,128,128]{3,2,1,0:T(8,128)S(1)}, f32[2,1,128,128]{3,2,1,0:T(8,128)S(1)}, u32[]{:S(2)}, u32[]{:S(2)}) collective-permute-start(f32[2,1,128,128]{3,2,1,0:T(8,128)S(1)} %get-tuple-element.47), channel_id=1, source_target_pairs={{0,1},{1,2},{2,3},{3,4},{4,5},{5,6},{6,7},{7,8},{8,9},{9,10},{10,1... | collective-permute-start | bytes 393224 | tf_op jit(solution)/shard_map/ppermute | solution.py:22
  146.3 2.7 fusion.19
  149.9 8.1 %collective-permute-start.22 = (f32[2,1,128,128]{3,2,1,0:T(8,128)}, f32[2,1,128,128]{3,2,1,0:T(8,128)}, u32[]{:S(2)}, u32[]{:S(2)}) collective-permute-start(f32[2,1,128,128]{3,2,1,0:T(8,128)} %get-tuple-element.44), channel_id=1, source_target_pairs={{0,1},{1,2},{2,3},{3,4},{4,5},{5,6},{6,7},{7,8},{8,9},{9,10},{10,1... | collective-permute-start | bytes 393224 | tf_op jit(solution)/shard_map/ppermute | solution.py:22
  160.9 2.1 copy.33
  163.0 1.4 collective-permute-done.23
  164.4 2.1 pad_multiply_fusion
  167.8 16.7 %copy.27 = f32[2,4,128,128]{0,3,2,1:T(8,128)} copy(f32[2,4,128,128]{3,2,1,0:T(8,128)S(1)} %fusion.35) | data formatting | bytes 1048576 | tf_op jit(solution)/shard_map/div | solution.py:79
  184.5 24.7 %gather_fusion = f32[4096,2]{1,0:T(8,128)} fusion(f32[2,65536]{0,1:T(8,128)} %bitcast.85, s32[4096]{0:T(1024)S(1)} %broadcast_clamp_fusion), kind=kCustom, calls=%fused_computation | custom fusion | bytes 81920 | tf_op jit(solution)/shard_map/jit(_take)/gather | solution.py:126
  209.1 4.3 fusion.1
  213.4 139.6 %psum.7 = f32[2,512]{0,1:T(8,128)S(1)} all-reduce(f32[2,512]{0,1:T(8,128)S(1)} %bitcast.96), channel_id=1, replica_groups=mesh['mem'=4,'space'=32] {'space'}, use_global_device_ids=true, to_apply=%region_2.3 | all-reduce | flops 1024 | bytes 8192 | tf_op jit(solution)/shard_map/psum | solution.py:128
  353.1 12.6 %all-gather = f32[4,2,512]{2,1,0:T(2,128)S(1)} all-gather(f32[1,2,512]{2,1,0:T(2,128)S(1)} %copy.30), channel_id=1, replica_groups=mesh['mem'=4,'space'=32] {'mem'}, dimensions={0}, use_global_device_ids=true | all-gather | bytes 20480 | tf_op jit(solution)/shard_map/all_gather | solution.py:129
  367.4 11.7 %cholesky.103 = f32[128,128]{1,0:T(8,128)S(1)} custom-call(f32[128,128]{1,0:T(8,128)S(1)} %cholesky.263), custom_call_target="Cholesky" | custom-call | tf_op jit(solution)/shard_map/jit(cholesky)/cholesky | solution.py:135
  379.3 9.8 %custom-call.32 = f32[1,128,128]{1,2,0:T(8,128)S(1)} custom-call(f32[1,128,128]{2,1,0:T(8,128)S(1)} %get-tuple-element.77), custom_call_target="InvertDiagBlocksLowerTriangular" | custom-call | tf_op jit(solution)/shard_map/jit(cholesky)/cholesky | solution.py:135
  389.8 11.7 %cholesky.215 = f32[128,128]{1,0:T(8,128)S(1)} custom-call(f32[128,128]{1,0:T(8,128)S(1)} %cholesky.267), custom_call_target="Cholesky" | custom-call | tf_op jit(solution)/shard_map/jit(cholesky)/cholesky | solution.py:135
  401.5 10.0 %custom-call.33 = f32[1,128,128]{1,2,0:T(8,128)S(1)} custom-call(f32[1,128,128]{2,1,0:T(8,128)S(1)} %get-tuple-element.74), custom_call_target="InvertDiagBlocksLowerTriangular" | custom-call | tf_op jit(solution)/shard_map/jit(cholesky)/cholesky | solution.py:135
  412.2 11.7 %cholesky.236 = f32[128,128]{1,0:T(8,128)S(1)} custom-call(f32[128,128]{1,0:T(8,128)S(1)} %cholesky.272), custom_call_target="Cholesky" | custom-call | tf_op jit(solution)/shard_map/jit(cholesky)/cholesky | solution.py:135
  424.6 9.8 %custom-call.34 = f32[1,128,128]{1,2,0:T(8,128)S(1)} custom-call(f32[1,128,128]{2,1,0:T(8,128)S(1)} %get-tuple-element.71), custom_call_target="InvertDiagBlocksLowerTriangular" | custom-call | tf_op jit(solution)/shard_map/jit(cholesky)/cholesky | solution.py:135
  435.0 11.9 %cholesky.253 = f32[128,128]{1,0:T(8,128)S(1)} custom-call(f32[128,128]{1,0:T(8,128)S(1)} %convolution_subtract_fusion.2), custom_call_target="Cholesky" | custom-call | tf_op jit(solution)/shard_map/jit(cholesky)/cholesky | solution.py:135
  451.0 10.5 %while.2 = (s32[]{:T(128)}, f32[512,512]{1,0:T(8,128)S(1)}, s32[4,2]{0,1:T(2,128)S(1)}, f32[4,128,128]{2,1,0:T(8,128)}) while((s32[]{:T(128)}, f32[512,512]{1,0:T(8,128)S(1)}, s32[4,2]{0,1:T(2,128)S(1)}, f32[4,128,128]{2,1,0:T(8,128)}) %tuple.55), condition=%wide.while_cond.clone, body=%wide.while_body.sunk.clone | while | flops 2 | bytes 132697 | solution.py:137
  451.7 2.0 bitcast_dynamic-update-slice_fusion.3
  454.3 2.0 bitcast_dynamic-update-slice_fusion.3
  456.9 2.0 bitcast_dynamic-update-slice_fusion.3
  459.6 2.0 bitcast_dynamic-update-slice_fusion.3
  461.5 40.1 %custom-call.35 = f32[4,128,128]{1,2,0:T(8,128)S(1)} custom-call(f32[4,128,128]{2,1,0:T(8,128)} %get-tuple-element.12), custom_call_target="InvertDiagBlocksLowerTriangular" | custom-call | tf_op jit(solution)/shard_map/triangular_solve | solution.py:137
  (180 shorter events, 60.7 us)
Async XLA Ops:
  0.0 2.2 copy-start.14
  2.2 3.5 copy-start.22
  2.2 3.5 copy-start.24
  3.0 3.8 collective-permute-start
  4.3 6.0 %collective-permute-start.1 = (f32[3,2,1,128,128]{4,3,2,1,0:T(8,128)S(1)}, f32[3,2,1,128,128]{4,3,2,1,0:T(8,128)}, u32[]{:S(2)}, u32[]{:S(2)}) collective-permute-start(f32[3,2,1,128,128]{4,3,2,1,0:T(8,128)S(1)} %get-tuple-element.31), channel_id=1, source_target_pairs={{1,0},{2,1},{3,2},{4,3},{5,4},{6,5},{7,6},{8,7},{9,8},{10,9},{11,1... | collective-permute-start | bytes 1179656 | tf_op jit(solution)/shard_map/ppermute | solution.py:24
  15.4 9.2 %collective-permute-start.2 = (f32[2,1,128,128]{3,2,1,0:T(8,128)S(1)}, f32[2,1,128,128]{3,2,1,0:T(8,128)S(1)}, u32[]{:S(2)}, u32[]{:S(2)}) collective-permute-start(f32[2,1,128,128]{3,2,1,0:T(8,128)S(1)} %get-tuple-element.64), channel_id=1, source_target_pairs={{0,1},{1,2},{2,3},{3,4},{4,5},{5,6},{6,7},{7,8},{8,9},{9,10},{10,1... | collective-permute-start | bytes 393224 | tf_op jit(solution)/shard_map/ppermute | solution.py:22
  23.2 3.2 collective-permute-start.3
  28.6 7.2 %collective-permute-start.4 = (f32[2,1,128,128]{3,2,1,0:T(8,128)S(1)}, f32[2,1,128,128]{3,2,1,0:T(8,128)S(1)}, u32[]{:S(2)}, u32[]{:S(2)}) collective-permute-start(f32[2,1,128,128]{3,2,1,0:T(8,128)S(1)} %get-tuple-element.62), channel_id=1, source_target_pairs={{1,0},{2,1},{3,2},{4,3},{5,4},{6,5},{7,6},{8,7},{9,8},{10,9},{11,1... | collective-permute-start | bytes 393224 | tf_op jit(solution)/shard_map/ppermute | solution.py:24
  29.9 6.8 %collective-permute-start.5 = (f32[2,1,128,128]{3,2,1,0:T(8,128)S(1)}, f32[2,1,128,128]{3,2,1,0:T(8,128)S(1)}, u32[]{:S(2)}, u32[]{:S(2)}) collective-permute-start(f32[2,1,128,128]{3,2,1,0:T(8,128)S(1)} %get-tuple-element.63), channel_id=1, source_target_pairs={{0,1},{1,2},{2,3},{3,4},{4,5},{5,6},{6,7},{7,8},{8,9},{9,10},{10,1... | collective-permute-start | bytes 393224 | tf_op jit(solution)/shard_map/ppermute | solution.py:22
  40.0 5.9 %collective-permute-start.6 = (f32[2,1,128,128]{3,2,1,0:T(8,128)S(1)}, f32[2,1,128,128]{3,2,1,0:T(8,128)S(1)}, u32[]{:S(2)}, u32[]{:S(2)}) collective-permute-start(f32[2,1,128,128]{3,2,1,0:T(8,128)S(1)} %get-tuple-element.60), channel_id=1, source_target_pairs={{0,1},{1,2},{2,3},{3,4},{4,5},{5,6},{6,7},{7,8},{8,9},{9,10},{10,1... | collective-permute-start | bytes 393224 | tf_op jit(solution)/shard_map/ppermute | solution.py:22
  44.7 5.2 %collective-permute-start.7 = (f32[2,1,128,128]{3,2,1,0:T(8,128)S(1)}, f32[2,1,128,128]{3,2,1,0:T(8,128)S(1)}, u32[]{:S(2)}, u32[]{:S(2)}) collective-permute-start(f32[2,1,128,128]{3,2,1,0:T(8,128)S(1)} %get-tuple-element.61), channel_id=1, source_target_pairs={{1,0},{2,1},{3,2},{4,3},{5,4},{6,5},{7,6},{8,7},{9,8},{10,9},{11,1... | collective-permute-start | bytes 393224 | tf_op jit(solution)/shard_map/ppermute | solution.py:24
  52.2 7.6 %collective-permute-start.8 = (f32[2,1,128,128]{3,2,1,0:T(8,128)S(1)}, f32[2,1,128,128]{3,2,1,0:T(8,128)S(1)}, u32[]{:S(2)}, u32[]{:S(2)}) collective-permute-start(f32[2,1,128,128]{3,2,1,0:T(8,128)S(1)} %get-tuple-element.58), channel_id=1, source_target_pairs={{1,0},{2,1},{3,2},{4,3},{5,4},{6,5},{7,6},{8,7},{9,8},{10,9},{11,1... | collective-permute-start | bytes 393224 | tf_op jit(solution)/shard_map/ppermute | solution.py:24
  53.5 7.1 %collective-permute-start.9 = (f32[2,1,128,128]{3,2,1,0:T(8,128)S(1)}, f32[2,1,128,128]{3,2,1,0:T(8,128)S(1)}, u32[]{:S(2)}, u32[]{:S(2)}) collective-permute-start(f32[2,1,128,128]{3,2,1,0:T(8,128)S(1)} %get-tuple-element.59), channel_id=1, source_target_pairs={{0,1},{1,2},{2,3},{3,4},{4,5},{5,6},{6,7},{7,8},{8,9},{9,10},{10,1... | collective-permute-start | bytes 393224 | tf_op jit(solution)/shard_map/ppermute | solution.py:22
  63.7 5.9 %collective-permute-start.10 = (f32[2,1,128,128]{3,2,1,0:T(8,128)S(1)}, f32[2,1,128,128]{3,2,1,0:T(8,128)S(1)}, u32[]{:S(2)}, u32[]{:S(2)}) collective-permute-start(f32[2,1,128,128]{3,2,1,0:T(8,128)S(1)} %get-tuple-element.56), channel_id=1, source_target_pairs={{0,1},{1,2},{2,3},{3,4},{4,5},{5,6},{6,7},{7,8},{8,9},{9,10},{10,1... | collective-permute-start | bytes 393224 | tf_op jit(solution)/shard_map/ppermute | solution.py:22
  68.3 5.2 %collective-permute-start.11 = (f32[2,1,128,128]{3,2,1,0:T(8,128)S(1)}, f32[2,1,128,128]{3,2,1,0:T(8,128)S(1)}, u32[]{:S(2)}, u32[]{:S(2)}) collective-permute-start(f32[2,1,128,128]{3,2,1,0:T(8,128)S(1)} %get-tuple-element.57), channel_id=1, source_target_pairs={{1,0},{2,1},{3,2},{4,3},{5,4},{6,5},{7,6},{8,7},{9,8},{10,9},{11,1... | collective-permute-start | bytes 393224 | tf_op jit(solution)/shard_map/ppermute | solution.py:24
  75.8 11.6 %copy-start.5 = (f32[2,4,128,128]{3,2,1,0:T(8,128)}, f32[2,4,128,128]{3,2,1,0:T(8,128)S(1)}, u32[]{:S(2)}) copy-start(f32[2,4,128,128]{3,2,1,0:T(8,128)S(1)} %fusion.137) | copy-start | bytes 1572868
  75.8 7.4 %collective-permute-start.12 = (f32[2,1,128,128]{3,2,1,0:T(8,128)S(1)}, f32[2,1,128,128]{3,2,1,0:T(8,128)S(1)}, u32[]{:S(2)}, u32[]{:S(2)}) collective-permute-start(f32[2,1,128,128]{3,2,1,0:T(8,128)S(1)} %get-tuple-element.54), channel_id=1, source_target_pairs={{1,0},{2,1},{3,2},{4,3},{5,4},{6,5},{7,6},{8,7},{9,8},{10,9},{11,1... | collective-permute-start | bytes 393224 | tf_op jit(solution)/shard_map/ppermute | solution.py:24
  77.1 7.1 %collective-permute-start.13 = (f32[2,1,128,128]{3,2,1,0:T(8,128)S(1)}, f32[2,1,128,128]{3,2,1,0:T(8,128)S(1)}, u32[]{:S(2)}, u32[]{:S(2)}) collective-permute-start(f32[2,1,128,128]{3,2,1,0:T(8,128)S(1)} %get-tuple-element.55), channel_id=1, source_target_pairs={{0,1},{1,2},{2,3},{3,4},{4,5},{5,6},{6,7},{7,8},{8,9},{9,10},{10,1... | collective-permute-start | bytes 393224 | tf_op jit(solution)/shard_map/ppermute | solution.py:22
  84.7 2.7 copy-start
  84.7 9.4 %copy-start.11 = (f32[2,4,128,128]{3,2,1,0:T(8,128)S(1)}, f32[2,4,128,128]{3,2,1,0:T(8,128)}, u32[]{:S(2)}) copy-start(f32[2,4,128,128]{3,2,1,0:T(8,128)} %param.10) | copy-start | bytes 1572868
  88.1 11.3 %collective-permute-start.14 = (f32[2,1,128,128]{3,2,1,0:T(8,128)S(1)}, f32[2,1,128,128]{3,2,1,0:T(8,128)S(1)}, u32[]{:S(2)}, u32[]{:S(2)}) collective-permute-start(f32[2,1,128,128]{3,2,1,0:T(8,128)S(1)} %get-tuple-element.52), channel_id=1, source_target_pairs={{0,1},{1,2},{2,3},{3,4},{4,5},{5,6},{6,7},{7,8},{8,9},{9,10},{10,1... | collective-permute-start | bytes 393224 | tf_op jit(solution)/shard_map/ppermute | solution.py:22
  92.7 7.4 %collective-permute-start.15 = (f32[2,1,128,128]{3,2,1,0:T(8,128)S(1)}, f32[2,1,128,128]{3,2,1,0:T(8,128)}, u32[]{:S(2)}, u32[]{:S(2)}) collective-permute-start(f32[2,1,128,128]{3,2,1,0:T(8,128)S(1)} %get-tuple-element.53), channel_id=1, source_target_pairs={{1,0},{2,1},{3,2},{4,3},{5,4},{6,5},{7,6},{8,7},{9,8},{10,9},{11,1... | collective-permute-start | bytes 393224 | tf_op jit(solution)/shard_map/ppermute | solution.py:24
  95.2 65.7 %all-to-all-start = ((f32[2,4,128,128]{3,1,0,2:T(4,128)}), f32[2,4,128,128]{3,1,0,2:T(4,128)}, u32[]{:S(2)}, u32[]{:S(2)}) async-start(f32[2,4,128,128]{3,1,0,2:T(4,128)} %copy.32), calls=%async_computation | async-start | bytes 1048576 | tf_op jit(solution)/shard_map/all_to_all | solution.py:142
  99.5 4.0 copy-start.1
  99.5 4.0 copy-start.6
  103.5 9.7 %copy-start.17 = (s32[512,8]{0,1:T(8,128)S(1)}, s32[512,8]{0,1:T(8,128)}, u32[]{:S(2)}) copy-start(s32[512,8]{0,1:T(8,128)} %param.15) | copy-start | bytes 49156
  104.9 0.8 copy-start.7
  106.4 9.4 %collective-permute-start.16 = (f32[2,1,128,128]{3,2,1,0:T(8,128)}, f32[2,1,128,128]{3,2,1,0:T(8,128)S(1)}, u32[]{:S(2)}, u32[]{:S(2)}) collective-permute-start(f32[2,1,128,128]{3,2,1,0:T(8,128)} %get-tuple-element.50), channel_id=1, source_target_pairs={{1,0},{2,1},{3,2},{4,3},{5,4},{6,5},{7,6},{8,7},{9,8},{10,9},{11,1... | collective-permute-start | bytes 393224 | tf_op jit(solution)/shard_map/ppermute | solution.py:24
  107.7 8.1 %collective-permute-start.17 = (f32[2,1,128,128]{3,2,1,0:T(8,128)}, f32[2,1,128,128]{3,2,1,0:T(8,128)S(1)}, u32[]{:S(2)}, u32[]{:S(2)}) collective-permute-start(f32[2,1,128,128]{3,2,1,0:T(8,128)} %get-tuple-element.51), channel_id=1, source_target_pairs={{0,1},{1,2},{2,3},{3,4},{4,5},{5,6},{6,7},{7,8},{8,9},{9,10},{10,1... | collective-permute-start | bytes 393224 | tf_op jit(solution)/shard_map/ppermute | solution.py:22
  115.7 1.7 copy-start.2
  115.8 1.7 copy-start.8
  117.5 9.4 %copy-start.19 = (f32[512,8]{0,1:T(8,128)S(1)}, f32[512,8]{0,1:T(8,128)}, u32[]{:S(2)}) copy-start(f32[512,8]{0,1:T(8,128)} %param.16) | copy-start | bytes 49156
  121.2 5.7 %collective-permute-start.18 = (f32[2,1,128,128]{3,2,1,0:T(8,128)S(1)}, f32[2,1,128,128]{3,2,1,0:T(8,128)S(1)}, u32[]{:S(2)}, u32[]{:S(2)}) collective-permute-start(f32[2,1,128,128]{3,2,1,0:T(8,128)S(1)} %get-tuple-element.48), channel_id=1, source_target_pairs={{0,1},{1,2},{2,3},{3,4},{4,5},{5,6},{6,7},{7,8},{8,9},{9,10},{10,1... | collective-permute-start | bytes 393224 | tf_op jit(solution)/shard_map/ppermute | solution.py:22
  125.2 8.4 %collective-permute-start.19 = (f32[2,1,128,128]{3,2,1,0:T(8,128)S(1)}, f32[2,1,128,128]{3,2,1,0:T(8,128)S(1)}, u32[]{:S(2)}, u32[]{:S(2)}) collective-permute-start(f32[2,1,128,128]{3,2,1,0:T(8,128)S(1)} %get-tuple-element.49), channel_id=1, source_target_pairs={{1,0},{2,1},{3,2},{4,3},{5,4},{6,5},{7,6},{8,7},{9,8},{10,9},{11,1... | collective-permute-start | bytes 393224 | tf_op jit(solution)/shard_map/ppermute | solution.py:24
  135.9 13.1 %copy-start.3 = (f32[2,4,128,128]{3,2,1,0:T(8,128)}, f32[2,4,128,128]{3,2,1,0:T(8,128)S(1)}, u32[]{:S(2)}) copy-start(f32[2,4,128,128]{3,2,1,0:T(8,128)S(1)} %fusion.69) | copy-start | bytes 1572868
  135.9 8.9 %collective-permute-start.20 = (f32[2,1,128,128]{3,2,1,0:T(8,128)S(1)}, f32[2,1,128,128]{3,2,1,0:T(8,128)S(1)}, u32[]{:S(2)}, u32[]{:S(2)}) collective-permute-start(f32[2,1,128,128]{3,2,1,0:T(8,128)S(1)} %get-tuple-element.46), channel_id=1, source_target_pairs={{1,0},{2,1},{3,2},{4,3},{5,4},{6,5},{7,6},{8,7},{9,8},{10,9},{11,1... | collective-permute-start | bytes 393224 | tf_op jit(solution)/shard_map/ppermute | solution.py:24
  137.2 8.5 %collective-permute-start.21 = (f32[2,1,128,128]{3,2,1,0:T(8,128)S(1)}, f32[2,1,128,128]{3,2,1,0:T(8,128)S(1)}, u32[]{:S(2)}, u32[]{:S(2)}) collective-permute-start(f32[2,1,128,128]{3,2,1,0:T(8,128)S(1)} %get-tuple-element.47), channel_id=1, source_target_pairs={{0,1},{1,2},{2,3},{3,4},{4,5},{5,6},{6,7},{7,8},{8,9},{9,10},{10,1... | collective-permute-start | bytes 393224 | tf_op jit(solution)/shard_map/ppermute | solution.py:22
  146.3 13.0 %copy-start.18 = (f32[512]{0:T(512)S(1)}, f32[512]{0:T(512)}, u32[]{:S(2)}) copy-start(f32[512]{0:T(512)} %param.18) | copy-start | bytes 6148
  146.3 13.0 %copy-start.20 = (pred[512,8]{0,1:T(8,128)(4,1)S(1)}, pred[512,8]{0,1:T(8,128)(4,1)}, u32[]{:S(2)}) copy-start(pred[512,8]{0,1:T(8,128)(4,1)} %get-tuple-element.21) | copy-start | bytes 12292
  149.0 0.9 copy-start.10
  149.9 13.1 %collective-permute-start.22 = (f32[2,1,128,128]{3,2,1,0:T(8,128)}, f32[2,1,128,128]{3,2,1,0:T(8,128)}, u32[]{:S(2)}, u32[]{:S(2)}) collective-permute-start(f32[2,1,128,128]{3,2,1,0:T(8,128)} %get-tuple-element.44), channel_id=1, source_target_pairs={{0,1},{1,2},{2,3},{3,4},{4,5},{5,6},{6,7},{7,8},{8,9},{9,10},{10,1... | collective-permute-start | bytes 393224 | tf_op jit(solution)/shard_map/ppermute | solution.py:22
  158.0 6.4 %collective-permute-start.23 = (f32[2,1,128,128]{3,2,1,0:T(8,128)}, f32[2,1,128,128]{3,2,1,0:T(8,128)}, u32[]{:S(2)}, u32[]{:S(2)}) collective-permute-start(f32[2,1,128,128]{3,2,1,0:T(8,128)} %get-tuple-element.45), channel_id=1, source_target_pairs={{1,0},{2,1},{3,2},{4,3},{5,4},{6,5},{7,6},{8,7},{9,8},{10,9},{11,1... | collective-permute-start | bytes 393224 | tf_op jit(solution)/shard_map/ppermute | solution.py:24
  163.0 3.4 copy-start.4
  184.4 24.7 %copy-start.13 = (f32[512,8]{1,0:T(8,128)S(1)}, f32[512,8]{1,0:T(8,128)}, u32[]{:S(2)}) copy-start(f32[512,8]{1,0:T(8,128)} %copy.29) | copy-start | bytes 49156
  184.4 24.7 %copy-start.15 = (pred[512,8]{1,0:T(8,128)(4,1)S(1)}, pred[512,8]{1,0:T(8,128)(4,1)}, u32[]{:S(2)}) copy-start(pred[512,8]{1,0:T(8,128)(4,1)} %copy.26) | copy-start | bytes 12292
  434.6 67.1 %copy-start.21 = (f32[8,512]{1,0:T(8,128)S(1)}, f32[8,512]{1,0:T(8,128)}, u32[]{:S(2)}) copy-start(f32[8,512]{1,0:T(8,128)} %param.19) | copy-start | bytes 49156
  434.6 67.1 %copy-start.23 = (f32[512]{0:T(512)S(1)}, f32[512]{0:T(512)}, u32[]{:S(2)}) copy-start(f32[512]{0:T(512)} %param.17) | copy-start | bytes 6148
  451.0 53.9 %copy-start.12 = (f32[2,4,4,32,128]{4,0,2,3,1:T(2,128)S(1)}, f32[2,4,4,32,128]{4,0,2,3,1:T(2,128)}, u32[]{:S(2)}) copy-start(f32[2,4,4,32,128]{4,0,2,3,1:T(2,128)} %copy.33) | copy-start | bytes 1572868
  (2 other events, 1.5 us)
where the time goes:
time: 516 us; the launch traced here: 507 us
  other arithmetic  166 us (32%)
  blocking collectives  152 us (29%)
  starting transfers between devices  86.5 us (17%)
  local copies, waits for them, and re-layouts  66.6 us (13%)
  waiting for transfers between devices  24.8 us (5%)
  matrix products  6.63 us (1%)
    psum x1, blocking collectives, body(): summed = lax.psum(partial_value, 'space')  140 us
    another operation x14, other arithmetic, body(): factor = jnp.linalg.cholesky(cov)  78.8 us
    ppermute x12, starting transfers between devices, padded(): lax.ppermute(tail, axis, [(i, (i + 1) % count) for i in range(ends)])  66.4 us
    another operation x3, other arithmetic, body(): lax.linalg.triangular_solve(factor, half, left_side=True, lower=True, tra...  40.2 us
    gather x1, local copies, waits for them, and re-layouts, body(): picked = jnp.take(flat, jnp.where(valid, local, 0), axis=1)  24.7 us
    ppermute x12, waiting for transfers between devices, padded(): lax.ppermute(head, axis, [((i + 1) % count, i) for i in range(ends)])  21.2 us
    min x6, other arithmetic, saturate(): return jnp.clip(middle(sat_pad) + time_step * (water - outflow), 0.0, 1.0)  16.8 us
    div x1, local copies, waits for them, and re-layouts, pressure(): return numer / denom  16.7 us
  transfers between devices with their start and end apart: 25, of which 10 were waited for; matrix products, arithmetic and copies ran while one was open for 5% of the time, Pallas kernels for 0%

commit v1 on v0

--- a/solution.py
+++ b/solution.py
@@ -125,7 +125,9 @@
     valid = (local >= 0) & (local < cells)
     picked = jnp.take(flat, jnp.where(valid, local, 0), axis=1)
     partial_value = jnp.sum(picked * jnp.where(valid, obs_weight, 0.0)[None], axis=2)
-    summed = lax.psum(partial_value, "space")
+    summed = partial_value
+    for hop in (1, 2, 4, 8, 16):
+        summed = summed + lax.ppermute(summed, "space", [(dev_, dev_ ^ hop) for dev_ in range(32)])
     predicted = lax.all_gather(summed, "mem", axis=0, tiled=True)
     ensemble = predicted.shape[0]
     high = lax.Precision.HIGHEST

time: 516 us -> 434 us (0.84)
  blocking collectives: 152 us -> 12.2 us
  starting transfers between devices: 86.5 us -> 126 us
  waiting for transfers between devices: 24.8 us -> 52.2 us
  local copies, waits for them, and re-layouts: 66.6 us -> 58.6 us
    psum x1 -> x0, blocking collectives: 140 us -> none  [body(): summed = lax.psum(partial_value, 'space')]
    ppermute x0 -> x5, starting transfers between devices: none -> 37.1 us  [body(): lax.ppermute(summed, 'space', [(dev_, dev_ ^ hop) for dev_ in range(32)])]
    ppermute x0 -> x5, waiting for transfers between devices: none -> 21.1 us  [body(): lax.ppermute(summed, 'space', [(dev_, dev_ ^ hop) for dev_ in range(32)])]
    ppermute x12, waiting for transfers between devices: 21.2 us -> 27 us  [padded(): lax.ppermute(head, axis, [((i + 1) % count, i) for i in range(ends)])]
  transfers between devices with their start and end apart: 25 -> 30, of which waited for: 10 -> 16; matrix products, arithmetic and copies ran while one was open for 5% -> 1% of each run, Pallas kernels for 0% -> 0%
where the time goes in v1:
time: 434 us; the launch traced here: 425 us
  other arithmetic  165 us (38%)
  starting transfers between devices  126 us (29%)
  local copies, waits for them, and re-layouts  58.6 us (14%)
  waiting for transfers between devices  52.2 us (12%)
  blocking collectives  12.2 us (3%)
  matrix products  6.63 us (2%)
    another operation x14, other arithmetic, body(): factor = jnp.linalg.cholesky(cov)  78.9 us
    ppermute x12, starting transfers between devices, padded(): lax.ppermute(tail, axis, [(i, (i + 1) % count) for i in range(ends)])  68.8 us
    another operation x3, other arithmetic, body(): lax.linalg.triangular_solve(factor, half, left_side=True, lower=True, tra...  39.4 us
    ppermute x5, starting transfers between devices, body(): lax.ppermute(summed, 'space', [(dev_, dev_ ^ hop) for dev_ in range(32)])  37.1 us
    ppermute x12, waiting for transfers between devices, padded(): lax.ppermute(head, axis, [((i + 1) % count, i) for i in range(ends)])  27 us
    gather x1, local copies, waits for them, and re-layouts, body(): picked = jnp.take(flat, jnp.where(valid, local, 0), axis=1)  21.3 us
    ppermute x5, waiting for transfers between devices, body(): lax.ppermute(summed, 'space', [(dev_, dev_ ^ hop) for dev_ in range(32)])  21.1 us
    min x6, other arithmetic, saturate(): return jnp.clip(middle(sat_pad) + time_step * (water - outflow), 0.0, 1.0)  18.1 us
  transfers between devices with their start and end apart: 30, of which 16 were waited for; matrix products, arithmetic and copies ran while one was open for 1% of the time, Pallas kernels for 0%

profile of v1, /device:TPU:0, one launch (start us, length us, event | category | flops | bytes accessed | tf_op | source)
XLA Modules:
  0.0 425.4 jit_solution(16498821443412667967)
XLA Ops:
  6.8 3.5 collective-permute-done.1
  12.6 2.6 fusion.189
  15.2 7.9 %collective-permute-start.2 = (f32[2,1,128,128]{3,2,1,0:T(8,128)S(1)}, f32[2,1,128,128]{3,2,1,0:T(8,128)S(1)}, u32[]{:S(2)}, u32[]{:S(2)}) collective-permute-start(f32[2,1,128,128]{3,2,1,0:T(8,128)S(1)} %get-tuple-element.64), channel_id=1, source_target_pairs={{0,1},{1,2},{2,3},{3,4},{4,5},{5,6},{6,7},{7,8},{8,9},{9,10},{10,1... | collective-permute-start | bytes 393224 | tf_op jit(solution)/shard_map/ppermute | solution.py:22
  24.4 1.9 collective-permute-done.3
  29.8 5.9 %collective-permute-start.5 = (f32[2,1,128,128]{3,2,1,0:T(8,128)S(1)}, f32[2,1,128,128]{3,2,1,0:T(8,128)S(1)}, u32[]{:S(2)}, u32[]{:S(2)}) collective-permute-start(f32[2,1,128,128]{3,2,1,0:T(8,128)S(1)} %get-tuple-element.63), channel_id=1, source_target_pairs={{0,1},{1,2},{2,3},{3,4},{4,5},{5,6},{6,7},{7,8},{8,9},{9,10},{10,1... | collective-permute-start | bytes 393224 | tf_op jit(solution)/shard_map/ppermute | solution.py:22
  37.2 2.7 fusion.155
  39.9 4.6 %collective-permute-start.6 = (f32[2,1,128,128]{3,2,1,0:T(8,128)S(1)}, f32[2,1,128,128]{3,2,1,0:T(8,128)S(1)}, u32[]{:S(2)}, u32[]{:S(2)}) collective-permute-start(f32[2,1,128,128]{3,2,1,0:T(8,128)S(1)} %get-tuple-element.60), channel_id=1, source_target_pairs={{0,1},{1,2},{2,3},{3,4},{4,5},{5,6},{6,7},{7,8},{8,9},{9,10},{10,1... | collective-permute-start | bytes 393224 | tf_op jit(solution)/shard_map/ppermute | solution.py:22
  45.8 3.9 collective-permute-done.7
  53.3 6.3 %collective-permute-start.9 = (f32[2,1,128,128]{3,2,1,0:T(8,128)S(1)}, f32[2,1,128,128]{3,2,1,0:T(8,128)S(1)}, u32[]{:S(2)}, u32[]{:S(2)}) collective-permute-start(f32[2,1,128,128]{3,2,1,0:T(8,128)S(1)} %get-tuple-element.59), channel_id=1, source_target_pairs={{0,1},{1,2},{2,3},{3,4},{4,5},{5,6},{6,7},{7,8},{8,9},{9,10},{10,1... | collective-permute-start | bytes 393224 | tf_op jit(solution)/shard_map/ppermute | solution.py:22
  60.9 2.6 fusion.121
  63.5 4.6 %collective-permute-start.10 = (f32[2,1,128,128]{3,2,1,0:T(8,128)S(1)}, f32[2,1,128,128]{3,2,1,0:T(8,128)S(1)}, u32[]{:S(2)}, u32[]{:S(2)}) collective-permute-start(f32[2,1,128,128]{3,2,1,0:T(8,128)S(1)} %get-tuple-element.56), channel_id=1, source_target_pairs={{0,1},{1,2},{2,3},{3,4},{4,5},{5,6},{6,7},{7,8},{8,9},{9,10},{10,1... | collective-permute-start | bytes 393224 | tf_op jit(solution)/shard_map/ppermute | solution.py:22
  69.4 3.9 collective-permute-done.11
  76.9 6.1 %collective-permute-start.13 = (f32[2,1,128,128]{3,2,1,0:T(8,128)S(1)}, f32[2,1,128,128]{3,2,1,0:T(8,128)S(1)}, u32[]{:S(2)}, u32[]{:S(2)}) collective-permute-start(f32[2,1,128,128]{3,2,1,0:T(8,128)S(1)} %get-tuple-element.55), channel_id=1, source_target_pairs={{0,1},{1,2},{2,3},{3,4},{4,5},{5,6},{6,7},{7,8},{8,9},{9,10},{10,1... | collective-permute-start | bytes 393224 | tf_op jit(solution)/shard_map/ppermute | solution.py:22
  84.5 2.6 fusion.87
  87.2 4.6 %collective-permute-start.14 = (f32[2,1,128,128]{3,2,1,0:T(8,128)S(1)}, f32[2,1,128,128]{3,2,1,0:T(8,128)S(1)}, u32[]{:S(2)}, u32[]{:S(2)}) collective-permute-start(f32[2,1,128,128]{3,2,1,0:T(8,128)S(1)} %get-tuple-element.52), channel_id=1, source_target_pairs={{0,1},{1,2},{2,3},{3,4},{4,5},{5,6},{6,7},{7,8},{8,9},{9,10},{10,1... | collective-permute-start | bytes 393224 | tf_op jit(solution)/shard_map/ppermute | solution.py:22
  93.1 3.9 collective-permute-done.15
  97.0 2.1 multiply_divide_fusion.1
  103.3 6.1 %collective-permute-start.17 = (f32[2,1,128,128]{3,2,1,0:T(8,128)}, f32[2,1,128,128]{3,2,1,0:T(8,128)S(1)}, u32[]{:S(2)}, u32[]{:S(2)}) collective-permute-start(f32[2,1,128,128]{3,2,1,0:T(8,128)} %get-tuple-element.51), channel_id=1, source_target_pairs={{0,1},{1,2},{2,3},{3,4},{4,5},{5,6},{6,7},{7,8},{8,9},{9,10},{10,1... | collective-permute-start | bytes 393224 | tf_op jit(solution)/shard_map/ppermute | solution.py:22
  112.1 3.9 fusion.53
  116.8 6.6 %collective-permute-start.18 = (f32[2,1,128,128]{3,2,1,0:T(8,128)S(1)}, f32[2,1,128,128]{3,2,1,0:T(8,128)S(1)}, u32[]{:S(2)}, u32[]{:S(2)}) collective-permute-start(f32[2,1,128,128]{3,2,1,0:T(8,128)S(1)} %get-tuple-element.48), channel_id=1, source_target_pairs={{0,1},{1,2},{2,3},{3,4},{4,5},{5,6},{6,7},{7,8},{8,9},{9,10},{10,1... | collective-permute-start | bytes 393224 | tf_op jit(solution)/shard_map/ppermute | solution.py:22
  126.8 3.9 collective-permute-done.19
  130.7 3.3 multiply_divide_fusion
  138.2 8.3 %collective-permute-start.21 = (f32[2,1,128,128]{3,2,1,0:T(8,128)}, f32[2,1,128,128]{3,2,1,0:T(8,128)S(1)}, u32[]{:S(2)}, u32[]{:S(2)}) collective-permute-start(f32[2,1,128,128]{3,2,1,0:T(8,128)} %get-tuple-element.47), channel_id=1, source_target_pairs={{0,1},{1,2},{2,3},{3,4},{4,5},{5,6},{6,7},{7,8},{8,9},{9,10},{10,1... | collective-permute-start | bytes 393224 | tf_op jit(solution)/shard_map/ppermute | solution.py:22
  149.3 3.7 fusion.19
  153.0 6.6 %collective-permute-start.22 = (f32[2,1,128,128]{3,2,1,0:T(8,128)S(1)}, f32[2,1,128,128]{3,2,1,0:T(8,128)S(1)}, u32[]{:S(2)}, u32[]{:S(2)}) collective-permute-start(f32[2,1,128,128]{3,2,1,0:T(8,128)S(1)} %get-tuple-element.44), channel_id=1, source_target_pairs={{0,1},{1,2},{2,3},{3,4},{4,5},{5,6},{6,7},{7,8},{8,9},{9,10},{10,1... | collective-permute-start | bytes 393224 | tf_op jit(solution)/shard_map/ppermute | solution.py:22
  160.9 6.1 %collective-permute-done.23 = f32[2,1,128,128]{3,2,1,0:T(8,128)S(1)} collective-permute-done((f32[2,1,128,128]{3,2,1,0:T(8,128)S(1)}, f32[2,1,128,128]{3,2,1,0:T(8,128)S(1)}, u32[]{:S(2)}, u32[]{:S(2)}) %collective-permute-start.23) | collective-permute-done | bytes 131104 | tf_op jit(solution)/shard_map/ppermute | solution.py:24
  169.3 16.7 %copy.27 = f32[2,4,128,128]{0,3,2,1:T(8,128)} copy(f32[2,4,128,128]{3,2,1,0:T(8,128)S(1)} %fusion.35) | data formatting | bytes 1048576 | tf_op jit(solution)/shard_map/div | solution.py:79
  186.0 21.3 %gather_fusion = f32[4096,2]{1,0:T(8,128)S(1)} fusion(f32[2,65536]{0,1:T(8,128)} %bitcast.87, s32[4096]{0:T(1024)S(1)} %broadcast_clamp_fusion), kind=kCustom, calls=%fused_computation | custom fusion | bytes 81920 | tf_op jit(solution)/shard_map/jit(_take)/gather | solution.py:126
  207.3 2.9 fusion.1
  210.2 5.6 %collective-permute-start.24 = (f32[2,512]{0,1:T(8,128)S(1)}, f32[2,512]{0,1:T(8,128)S(1)}, u32[]{:S(2)}, u32[]{:S(2)}) collective-permute-start(f32[2,512]{0,1:T(8,128)S(1)} %bitcast.98), channel_id=1, source_target_pairs={{0,1},{1,0},{2,3},{3,2},{4,5},{5,4},{6,7},{7,6},{8,9},{9,8},{10,11... | collective-permute-start | bytes 12296 | tf_op jit(solution)/shard_map/ppermute | solution.py:130
  217.0 4.4 %all-to-all-start = ((f32[2,4,128,128]{3,1,0,2:T(4,128)}), f32[2,4,128,128]{3,1,0,2:T(4,128)S(1)}, u32[]{:S(2)}, u32[]{:S(2)}) async-start(f32[2,4,128,128]{3,1,0,2:T(4,128)} %copy.32), calls=%async_computation | async-start | bytes 1048576 | tf_op jit(solution)/shard_map/all_to_all | solution.py:144
  221.4 9.3 %collective-permute-start.25 = (f32[2,512]{0,1:T(8,128)S(1)}, f32[2,512]{0,1:T(8,128)S(1)}, u32[]{:S(2)}, u32[]{:S(2)}) collective-permute-start(f32[2,512]{0,1:T(8,128)S(1)} %bitcast_add_fusion), channel_id=1, source_target_pairs={{0,2},{1,3},{2,0},{3,1},{4,6},{5,7},{6,4},{7,5},{8,10},{9,11},{10,... | collective-permute-start | bytes 12296 | tf_op jit(solution)/shard_map/ppermute | solution.py:130
  230.7 6.2 %collective-permute-done.25 = f32[2,512]{0,1:T(8,128)S(1)} collective-permute-done((f32[2,512]{0,1:T(8,128)S(1)}, f32[2,512]{0,1:T(8,128)S(1)}, u32[]{:S(2)}, u32[]{:S(2)}) %collective-permute-start.25) | collective-permute-done | bytes 4128 | tf_op jit(solution)/shard_map/ppermute | solution.py:130
  237.0 17.7 %collective-permute-start.26 = (f32[2,512]{0,1:T(8,128)S(1)}, f32[2,512]{0,1:T(8,128)S(1)}, u32[]{:S(2)}, u32[]{:S(2)}) collective-permute-start(f32[2,512]{0,1:T(8,128)S(1)} %add.1001), channel_id=1, source_target_pairs={{0,4},{1,5},{2,6},{3,7},{4,0},{5,1},{6,2},{7,3},{8,12},{9,13},{10,... | collective-permute-start | bytes 12296 | tf_op jit(solution)/shard_map/ppermute | solution.py:130
  254.6 5.6 %collective-permute-done.26 = f32[2,512]{0,1:T(8,128)S(1)} collective-permute-done((f32[2,512]{0,1:T(8,128)S(1)}, f32[2,512]{0,1:T(8,128)S(1)}, u32[]{:S(2)}, u32[]{:S(2)}) %collective-permute-start.26) | collective-permute-done | bytes 4128 | tf_op jit(solution)/shard_map/ppermute | solution.py:130
  262.0 5.2 %collective-permute-done.27 = f32[2,512]{0,1:T(8,128)S(1)} collective-permute-done((f32[2,512]{0,1:T(8,128)S(1)}, f32[2,512]{0,1:T(8,128)S(1)}, u32[]{:S(2)}, u32[]{:S(2)}) %collective-permute-start.27) | collective-permute-done | bytes 4128 | tf_op jit(solution)/shard_map/ppermute | solution.py:130
  267.2 2.9 collective-permute-start.28
  271.2 4.0 collective-permute-done.28
  275.3 12.2 %all-gather = f32[4,2,512]{2,1,0:T(2,128)S(1)} all-gather(f32[1,2,512]{2,1,0:T(2,128)S(1)} %copy.30), channel_id=1, replica_groups=mesh['mem'=4,'space'=32] {'mem'}, dimensions={0}, use_global_device_ids=true | all-gather | bytes 20480 | tf_op jit(solution)/shard_map/all_gather | solution.py:131
  289.2 11.7 %cholesky.103 = f32[128,128]{1,0:T(8,128)S(1)} custom-call(f32[128,128]{1,0:T(8,128)S(1)} %cholesky.263), custom_call_target="Cholesky" | custom-call | tf_op jit(solution)/shard_map/jit(cholesky)/cholesky | solution.py:137
  301.1 9.8 %custom-call.32 = f32[1,128,128]{1,2,0:T(8,128)S(1)} custom-call(f32[1,128,128]{2,1,0:T(8,128)S(1)} %get-tuple-element.77), custom_call_target="InvertDiagBlocksLowerTriangular" | custom-call | tf_op jit(solution)/shard_map/jit(cholesky)/cholesky | solution.py:137
  311.6 11.7 %cholesky.215 = f32[128,128]{1,0:T(8,128)S(1)} custom-call(f32[128,128]{1,0:T(8,128)S(1)} %cholesky.267), custom_call_target="Cholesky" | custom-call | tf_op jit(solution)/shard_map/jit(cholesky)/cholesky | solution.py:137
  323.3 10.0 %custom-call.33 = f32[1,128,128]{1,2,0:T(8,128)S(1)} custom-call(f32[1,128,128]{2,1,0:T(8,128)S(1)} %get-tuple-element.74), custom_call_target="InvertDiagBlocksLowerTriangular" | custom-call | tf_op jit(solution)/shard_map/jit(cholesky)/cholesky | solution.py:137
  334.0 11.7 %cholesky.236 = f32[128,128]{1,0:T(8,128)S(1)} custom-call(f32[128,128]{1,0:T(8,128)S(1)} %cholesky.272), custom_call_target="Cholesky" | custom-call | tf_op jit(solution)/shard_map/jit(cholesky)/cholesky | solution.py:137
  346.4 9.8 %custom-call.34 = f32[1,128,128]{1,2,0:T(8,128)S(1)} custom-call(f32[1,128,128]{2,1,0:T(8,128)S(1)} %get-tuple-element.71), custom_call_target="InvertDiagBlocksLowerTriangular" | custom-call | tf_op jit(solution)/shard_map/jit(cholesky)/cholesky | solution.py:137
  356.8 11.9 %cholesky.253 = f32[128,128]{1,0:T(8,128)S(1)} custom-call(f32[128,128]{1,0:T(8,128)S(1)} %convolution_subtract_fusion.2), custom_call_target="Cholesky" | custom-call | tf_op jit(solution)/shard_map/jit(cholesky)/cholesky | solution.py:137
  372.9 8.1 %while.2 = (s32[]{:T(128)}, f32[512,512]{1,0:T(8,128)S(1)}, s32[4,2]{0,1:T(2,128)S(1)}, f32[4,128,128]{2,1,0:T(8,128)S(1)}) while((s32[]{:T(128)}, f32[512,512]{1,0:T(8,128)S(1)}, s32[4,2]{0,1:T(2,128)S(1)}, f32[4,128,128]{2,1,0:T(8,128)S(1)}) %tuple.55), condition=%wide.while_cond.clone, body=%wide.while_body.sunk.clone | while | flops 2 | bytes 131173 | solution.py:139
  380.9 39.3 %custom-call.35 = f32[4,128,128]{1,2,0:T(8,128)S(1)} custom-call(f32[4,128,128]{2,1,0:T(8,128)S(1)} %get-tuple-element.12), custom_call_target="InvertDiagBlocksLowerTriangular" | custom-call | tf_op jit(solution)/shard_map/triangular_solve | solution.py:139
  (192 shorter events, 73.3 us)
Async XLA Ops:
  0.0 2.2 copy-start.14
  2.2 3.5 copy-start.21
  2.2 3.5 copy-start.23
  3.0 3.8 collective-permute-start
  4.3 6.0 %collective-permute-start.1 = (f32[3,2,1,128,128]{4,3,2,1,0:T(8,128)S(1)}, f32[3,2,1,128,128]{4,3,2,1,0:T(8,128)}, u32[]{:S(2)}, u32[]{:S(2)}) collective-permute-start(f32[3,2,1,128,128]{4,3,2,1,0:T(8,128)S(1)} %get-tuple-element.31), channel_id=1, source_target_pairs={{1,0},{2,1},{3,2},{4,3},{5,4},{6,5},{7,6},{8,7},{9,8},{10,9},{11,1... | collective-permute-start | bytes 1179656 | tf_op jit(solution)/shard_map/ppermute | solution.py:24
  15.2 9.2 %collective-permute-start.2 = (f32[2,1,128,128]{3,2,1,0:T(8,128)S(1)}, f32[2,1,128,128]{3,2,1,0:T(8,128)S(1)}, u32[]{:S(2)}, u32[]{:S(2)}) collective-permute-start(f32[2,1,128,128]{3,2,1,0:T(8,128)S(1)} %get-tuple-element.64), channel_id=1, source_target_pairs={{0,1},{1,2},{2,3},{3,4},{4,5},{5,6},{6,7},{7,8},{8,9},{9,10},{10,1... | collective-permute-start | bytes 393224 | tf_op jit(solution)/shard_map/ppermute | solution.py:22
  23.1 3.2 collective-permute-start.3
  28.5 7.2 %collective-permute-start.4 = (f32[2,1,128,128]{3,2,1,0:T(8,128)S(1)}, f32[2,1,128,128]{3,2,1,0:T(8,128)S(1)}, u32[]{:S(2)}, u32[]{:S(2)}) collective-permute-start(f32[2,1,128,128]{3,2,1,0:T(8,128)S(1)} %get-tuple-element.62), channel_id=1, source_target_pairs={{1,0},{2,1},{3,2},{4,3},{5,4},{6,5},{7,6},{8,7},{9,8},{10,9},{11,1... | collective-permute-start | bytes 393224 | tf_op jit(solution)/shard_map/ppermute | solution.py:24
  29.8 6.8 %collective-permute-start.5 = (f32[2,1,128,128]{3,2,1,0:T(8,128)S(1)}, f32[2,1,128,128]{3,2,1,0:T(8,128)S(1)}, u32[]{:S(2)}, u32[]{:S(2)}) collective-permute-start(f32[2,1,128,128]{3,2,1,0:T(8,128)S(1)} %get-tuple-element.63), channel_id=1, source_target_pairs={{0,1},{1,2},{2,3},{3,4},{4,5},{5,6},{6,7},{7,8},{8,9},{9,10},{10,1... | collective-permute-start | bytes 393224 | tf_op jit(solution)/shard_map/ppermute | solution.py:22
  39.9 5.9 %collective-permute-start.6 = (f32[2,1,128,128]{3,2,1,0:T(8,128)S(1)}, f32[2,1,128,128]{3,2,1,0:T(8,128)S(1)}, u32[]{:S(2)}, u32[]{:S(2)}) collective-permute-start(f32[2,1,128,128]{3,2,1,0:T(8,128)S(1)} %get-tuple-element.60), channel_id=1, source_target_pairs={{0,1},{1,2},{2,3},{3,4},{4,5},{5,6},{6,7},{7,8},{8,9},{9,10},{10,1... | collective-permute-start | bytes 393224 | tf_op jit(solution)/shard_map/ppermute | solution.py:22
  44.5 5.2 %collective-permute-start.7 = (f32[2,1,128,128]{3,2,1,0:T(8,128)S(1)}, f32[2,1,128,128]{3,2,1,0:T(8,128)S(1)}, u32[]{:S(2)}, u32[]{:S(2)}) collective-permute-start(f32[2,1,128,128]{3,2,1,0:T(8,128)S(1)} %get-tuple-element.61), channel_id=1, source_target_pairs={{1,0},{2,1},{3,2},{4,3},{5,4},{6,5},{7,6},{8,7},{9,8},{10,9},{11,1... | collective-permute-start | bytes 393224 | tf_op jit(solution)/shard_map/ppermute | solution.py:24
  52.0 7.6 %collective-permute-start.8 = (f32[2,1,128,128]{3,2,1,0:T(8,128)S(1)}, f32[2,1,128,128]{3,2,1,0:T(8,128)S(1)}, u32[]{:S(2)}, u32[]{:S(2)}) collective-permute-start(f32[2,1,128,128]{3,2,1,0:T(8,128)S(1)} %get-tuple-element.58), channel_id=1, source_target_pairs={{1,0},{2,1},{3,2},{4,3},{5,4},{6,5},{7,6},{8,7},{9,8},{10,9},{11,1... | collective-permute-start | bytes 393224 | tf_op jit(solution)/shard_map/ppermute | solution.py:24
  53.3 7.1 %collective-permute-start.9 = (f32[2,1,128,128]{3,2,1,0:T(8,128)S(1)}, f32[2,1,128,128]{3,2,1,0:T(8,128)S(1)}, u32[]{:S(2)}, u32[]{:S(2)}) collective-permute-start(f32[2,1,128,128]{3,2,1,0:T(8,128)S(1)} %get-tuple-element.59), channel_id=1, source_target_pairs={{0,1},{1,2},{2,3},{3,4},{4,5},{5,6},{6,7},{7,8},{8,9},{9,10},{10,1... | collective-permute-start | bytes 393224 | tf_op jit(solution)/shard_map/ppermute | solution.py:22
  63.5 5.9 %collective-permute-start.10 = (f32[2,1,128,128]{3,2,1,0:T(8,128)S(1)}, f32[2,1,128,128]{3,2,1,0:T(8,128)S(1)}, u32[]{:S(2)}, u32[]{:S(2)}) collective-permute-start(f32[2,1,128,128]{3,2,1,0:T(8,128)S(1)} %get-tuple-element.56), channel_id=1, source_target_pairs={{0,1},{1,2},{2,3},{3,4},{4,5},{5,6},{6,7},{7,8},{8,9},{9,10},{10,1... | collective-permute-start | bytes 393224 | tf_op jit(solution)/shard_map/ppermute | solution.py:22
  68.1 5.2 %collective-permute-start.11 = (f32[2,1,128,128]{3,2,1,0:T(8,128)S(1)}, f32[2,1,128,128]{3,2,1,0:T(8,128)S(1)}, u32[]{:S(2)}, u32[]{:S(2)}) collective-permute-start(f32[2,1,128,128]{3,2,1,0:T(8,128)S(1)} %get-tuple-element.57), channel_id=1, source_target_pairs={{1,0},{2,1},{3,2},{4,3},{5,4},{6,5},{7,6},{8,7},{9,8},{10,9},{11,1... | collective-permute-start | bytes 393224 | tf_op jit(solution)/shard_map/ppermute | solution.py:24
  75.6 7.4 %collective-permute-start.12 = (f32[2,1,128,128]{3,2,1,0:T(8,128)S(1)}, f32[2,1,128,128]{3,2,1,0:T(8,128)S(1)}, u32[]{:S(2)}, u32[]{:S(2)}) collective-permute-start(f32[2,1,128,128]{3,2,1,0:T(8,128)S(1)} %get-tuple-element.54), channel_id=1, source_target_pairs={{1,0},{2,1},{3,2},{4,3},{5,4},{6,5},{7,6},{8,7},{9,8},{10,9},{11,1... | collective-permute-start | bytes 393224 | tf_op jit(solution)/shard_map/ppermute | solution.py:24
  76.9 7.1 %collective-permute-start.13 = (f32[2,1,128,128]{3,2,1,0:T(8,128)S(1)}, f32[2,1,128,128]{3,2,1,0:T(8,128)S(1)}, u32[]{:S(2)}, u32[]{:S(2)}) collective-permute-start(f32[2,1,128,128]{3,2,1,0:T(8,128)S(1)} %get-tuple-element.55), channel_id=1, source_target_pairs={{0,1},{1,2},{2,3},{3,4},{4,5},{5,6},{6,7},{7,8},{8,9},{9,10},{10,1... | collective-permute-start | bytes 393224 | tf_op jit(solution)/shard_map/ppermute | solution.py:22
  87.1 12.0 %copy-start.10 = (f32[2,4,128,128]{3,2,1,0:T(8,128)}, f32[2,4,128,128]{3,2,1,0:T(8,128)S(1)}, u32[]{:S(2)}) copy-start(f32[2,4,128,128]{3,2,1,0:T(8,128)S(1)} %fusion.87) | copy-start | bytes 1572868
  87.2 5.9 %collective-permute-start.14 = (f32[2,1,128,128]{3,2,1,0:T(8,128)S(1)}, f32[2,1,128,128]{3,2,1,0:T(8,128)S(1)}, u32[]{:S(2)}, u32[]{:S(2)}) collective-permute-start(f32[2,1,128,128]{3,2,1,0:T(8,128)S(1)} %get-tuple-element.52), channel_id=1, source_target_pairs={{0,1},{1,2},{2,3},{3,4},{4,5},{5,6},{6,7},{7,8},{8,9},{9,10},{10,1... | collective-permute-start | bytes 393224 | tf_op jit(solution)/shard_map/ppermute | solution.py:22
  91.8 5.2 %collective-permute-start.15 = (f32[2,1,128,128]{3,2,1,0:T(8,128)S(1)}, f32[2,1,128,128]{3,2,1,0:T(8,128)S(1)}, u32[]{:S(2)}, u32[]{:S(2)}) collective-permute-start(f32[2,1,128,128]{3,2,1,0:T(8,128)S(1)} %get-tuple-element.53), channel_id=1, source_target_pairs={{1,0},{2,1},{3,2},{4,3},{5,4},{6,5},{7,6},{8,7},{9,8},{10,9},{11,1... | collective-permute-start | bytes 393224 | tf_op jit(solution)/shard_map/ppermute | solution.py:24
  102.0 7.4 %collective-permute-start.16 = (f32[2,1,128,128]{3,2,1,0:T(8,128)}, f32[2,1,128,128]{3,2,1,0:T(8,128)S(1)}, u32[]{:S(2)}, u32[]{:S(2)}) collective-permute-start(f32[2,1,128,128]{3,2,1,0:T(8,128)} %get-tuple-element.50), channel_id=1, source_target_pairs={{1,0},{2,1},{3,2},{4,3},{5,4},{6,5},{7,6},{8,7},{9,8},{10,9},{11,1... | collective-permute-start | bytes 393224 | tf_op jit(solution)/shard_map/ppermute | solution.py:24
  103.3 7.3 %collective-permute-start.17 = (f32[2,1,128,128]{3,2,1,0:T(8,128)}, f32[2,1,128,128]{3,2,1,0:T(8,128)S(1)}, u32[]{:S(2)}, u32[]{:S(2)}) collective-permute-start(f32[2,1,128,128]{3,2,1,0:T(8,128)} %get-tuple-element.51), channel_id=1, source_target_pairs={{0,1},{1,2},{2,3},{3,4},{4,5},{5,6},{6,7},{7,8},{8,9},{9,10},{10,1... | collective-permute-start | bytes 393224 | tf_op jit(solution)/shard_map/ppermute | solution.py:22
  109.4 2.7 copy-start.3
  109.4 2.7 copy-start.5
  112.1 3.9 copy-start
  112.1 13.0 %copy-start.17 = (s32[512,8]{0,1:T(8,128)S(1)}, s32[512,8]{0,1:T(8,128)}, u32[]{:S(2)}) copy-start(s32[512,8]{0,1:T(8,128)} %param.15) | copy-start | bytes 49156
  116.8 9.4 %collective-permute-start.18 = (f32[2,1,128,128]{3,2,1,0:T(8,128)S(1)}, f32[2,1,128,128]{3,2,1,0:T(8,128)S(1)}, u32[]{:S(2)}, u32[]{:S(2)}) collective-permute-start(f32[2,1,128,128]{3,2,1,0:T(8,128)S(1)} %get-tuple-element.48), channel_id=1, source_target_pairs={{0,1},{1,2},{2,3},{3,4},{4,5},{5,6},{6,7},{7,8},{8,9},{9,10},{10,1... | collective-permute-start | bytes 393224 | tf_op jit(solution)/shard_map/ppermute | solution.py:22
  123.4 7.3 %collective-permute-start.19 = (f32[2,1,128,128]{3,2,1,0:T(8,128)S(1)}, f32[2,1,128,128]{3,2,1,0:T(8,128)}, u32[]{:S(2)}, u32[]{:S(2)}) collective-permute-start(f32[2,1,128,128]{3,2,1,0:T(8,128)S(1)} %get-tuple-element.49), channel_id=1, source_target_pairs={{1,0},{2,1},{3,2},{4,3},{5,4},{6,5},{7,6},{8,7},{9,8},{10,9},{11,1... | collective-permute-start | bytes 393224 | tf_op jit(solution)/shard_map/ppermute | solution.py:24
  126.2 7.8 %copy-start.1 = (f32[2,6,130,130]{3,2,1,0:T(8,128)S(1)}, f32[2,6,130,130]{3,2,1,0:T(8,128)}, u32[]{:S(2)}) copy-start(f32[2,6,130,130]{3,2,1,0:T(8,128)} %copy-done) | copy-start | bytes 2433604
  126.2 7.8 %copy-start.6 = (f32[2,4,128,128]{3,2,1,0:T(8,128)S(1)}, f32[2,4,128,128]{3,2,1,0:T(8,128)}, u32[]{:S(2)}) copy-start(f32[2,4,128,128]{3,2,1,0:T(8,128)} %copy-done.4) | copy-start | bytes 1572868
  134.0 12.5 %copy-start.19 = (f32[512,8]{0,1:T(8,128)S(1)}, f32[512,8]{0,1:T(8,128)}, u32[]{:S(2)}) copy-start(f32[512,8]{0,1:T(8,128)} %param.16) | copy-start | bytes 49156
  136.9 10.5 %collective-permute-start.20 = (f32[2,1,128,128]{3,2,1,0:T(8,128)}, f32[2,1,128,128]{3,2,1,0:T(8,128)S(1)}, u32[]{:S(2)}, u32[]{:S(2)}) collective-permute-start(f32[2,1,128,128]{3,2,1,0:T(8,128)} %get-tuple-element.46), channel_id=1, source_target_pairs={{1,0},{2,1},{3,2},{4,3},{5,4},{6,5},{7,6},{8,7},{9,8},{10,9},{11,1... | collective-permute-start | bytes 393224 | tf_op jit(solution)/shard_map/ppermute | solution.py:24
  138.2 9.4 %collective-permute-start.21 = (f32[2,1,128,128]{3,2,1,0:T(8,128)}, f32[2,1,128,128]{3,2,1,0:T(8,128)S(1)}, u32[]{:S(2)}, u32[]{:S(2)}) collective-permute-start(f32[2,1,128,128]{3,2,1,0:T(8,128)} %get-tuple-element.47), channel_id=1, source_target_pairs={{0,1},{1,2},{2,3},{3,4},{4,5},{5,6},{6,7},{7,8},{8,9},{9,10},{10,1... | collective-permute-start | bytes 393224 | tf_op jit(solution)/shard_map/ppermute | solution.py:22
  153.0 7.9 %collective-permute-start.22 = (f32[2,1,128,128]{3,2,1,0:T(8,128)S(1)}, f32[2,1,128,128]{3,2,1,0:T(8,128)S(1)}, u32[]{:S(2)}, u32[]{:S(2)}) collective-permute-start(f32[2,1,128,128]{3,2,1,0:T(8,128)S(1)} %get-tuple-element.44), channel_id=1, source_target_pairs={{0,1},{1,2},{2,3},{3,4},{4,5},{5,6},{6,7},{7,8},{8,9},{9,10},{10,1... | collective-permute-start | bytes 393224 | tf_op jit(solution)/shard_map/ppermute | solution.py:22
  159.6 7.4 %collective-permute-start.23 = (f32[2,1,128,128]{3,2,1,0:T(8,128)S(1)}, f32[2,1,128,128]{3,2,1,0:T(8,128)S(1)}, u32[]{:S(2)}, u32[]{:S(2)}) collective-permute-start(f32[2,1,128,128]{3,2,1,0:T(8,128)S(1)} %get-tuple-element.45), channel_id=1, source_target_pairs={{1,0},{2,1},{3,2},{4,3},{5,4},{6,5},{7,6},{8,7},{9,8},{10,9},{11,1... | collective-permute-start | bytes 393224 | tf_op jit(solution)/shard_map/ppermute | solution.py:24
  186.0 21.4 %copy-start.13 = (f32[512,8]{1,0:T(8,128)S(1)}, f32[512,8]{1,0:T(8,128)}, u32[]{:S(2)}) copy-start(f32[512,8]{1,0:T(8,128)} %copy.29) | copy-start | bytes 49156
  186.0 21.4 %copy-start.15 = (pred[512,8]{1,0:T(8,128)(4,1)S(1)}, pred[512,8]{1,0:T(8,128)(4,1)}, u32[]{:S(2)}) copy-start(pred[512,8]{1,0:T(8,128)(4,1)} %copy.26) | copy-start | bytes 12292
  207.3 8.5 %copy-start.11 = (f32[2,4,128,128]{3,2,1,0:T(8,128)S(1)}, f32[2,4,128,128]{3,2,1,0:T(8,128)}, u32[]{:S(2)}) copy-start(f32[2,4,128,128]{3,2,1,0:T(8,128)} %param.10) | copy-start | bytes 1572868
  210.2 11.2 %collective-permute-start.24 = (f32[2,512]{0,1:T(8,128)S(1)}, f32[2,512]{0,1:T(8,128)S(1)}, u32[]{:S(2)}, u32[]{:S(2)}) collective-permute-start(f32[2,512]{0,1:T(8,128)S(1)} %bitcast.98), channel_id=1, source_target_pairs={{0,1},{1,0},{2,3},{3,2},{4,5},{5,4},{6,7},{7,6},{8,9},{9,8},{10,11... | collective-permute-start | bytes 12296 | tf_op jit(solution)/shard_map/ppermute | solution.py:130
  217.0 45.0 %copy-start.18 = (f32[512]{0:T(512)S(1)}, f32[512]{0:T(512)}, u32[]{:S(2)}) copy-start(f32[512]{0:T(512)} %param.18) | copy-start | bytes 6148
  217.0 53.2 %all-to-all-start = ((f32[2,4,128,128]{3,1,0,2:T(4,128)}), f32[2,4,128,128]{3,1,0,2:T(4,128)S(1)}, u32[]{:S(2)}, u32[]{:S(2)}) async-start(f32[2,4,128,128]{3,1,0,2:T(4,128)} %copy.32), calls=%async_computation | async-start | bytes 1048576 | tf_op jit(solution)/shard_map/all_to_all | solution.py:144
  221.4 15.5 %collective-permute-start.25 = (f32[2,512]{0,1:T(8,128)S(1)}, f32[2,512]{0,1:T(8,128)S(1)}, u32[]{:S(2)}, u32[]{:S(2)}) collective-permute-start(f32[2,512]{0,1:T(8,128)S(1)} %bitcast_add_fusion), channel_id=1, source_target_pairs={{0,2},{1,3},{2,0},{3,1},{4,6},{5,7},{6,4},{7,5},{8,10},{9,11},{10,... | collective-permute-start | bytes 12296 | tf_op jit(solution)/shard_map/ppermute | solution.py:130
  237.0 23.3 %collective-permute-start.26 = (f32[2,512]{0,1:T(8,128)S(1)}, f32[2,512]{0,1:T(8,128)S(1)}, u32[]{:S(2)}, u32[]{:S(2)}) collective-permute-start(f32[2,512]{0,1:T(8,128)S(1)} %add.1001), channel_id=1, source_target_pairs={{0,4},{1,5},{2,6},{3,7},{4,0},{5,1},{6,2},{7,3},{8,12},{9,13},{10,... | collective-permute-start | bytes 12296 | tf_op jit(solution)/shard_map/ppermute | solution.py:130
  260.3 6.9 %collective-permute-start.27 = (f32[2,512]{0,1:T(8,128)S(1)}, f32[2,512]{0,1:T(8,128)S(1)}, u32[]{:S(2)}, u32[]{:S(2)}) collective-permute-start(f32[2,512]{0,1:T(8,128)S(1)} %add.1002), channel_id=1, source_target_pairs={{0,8},{1,9},{2,10},{3,11},{4,12},{5,13},{6,14},{7,15},{8,0},{9,1},... | collective-permute-start | bytes 12296 | tf_op jit(solution)/shard_map/ppermute | solution.py:130
  267.2 8.0 %collective-permute-start.28 = (f32[2,512]{0,1:T(8,128)S(1)}, f32[2,512]{0,1:T(8,128)S(1)}, u32[]{:S(2)}, u32[]{:S(2)}) collective-permute-start(f32[2,512]{0,1:T(8,128)S(1)} %add.1003), channel_id=1, source_target_pairs={{0,16},{1,17},{2,18},{3,19},{4,20},{5,21},{6,22},{7,23},{8,24},{9,... | collective-permute-start | bytes 12296 | tf_op jit(solution)/shard_map/ppermute | solution.py:130
  356.4 63.8 %copy-start.20 = (f32[8,512]{1,0:T(8,128)S(1)}, f32[8,512]{1,0:T(8,128)}, u32[]{:S(2)}) copy-start(f32[8,512]{1,0:T(8,128)} %param.19) | copy-start | bytes 49156
  356.4 63.8 %copy-start.22 = (f32[512]{0:T(512)S(1)}, f32[512]{0:T(512)}, u32[]{:S(2)}) copy-start(f32[512]{0:T(512)} %param.17) | copy-start | bytes 6148
  372.8 50.6 %copy-start.12 = (f32[2,4,4,32,128]{4,0,2,3,1:T(2,128)S(1)}, f32[2,4,4,32,128]{4,0,2,3,1:T(2,128)}, u32[]{:S(2)}) copy-start(f32[2,4,4,32,128]{4,0,2,3,1:T(2,128)} %copy.33) | copy-start | bytes 1572868
  (6 other events, 7.0 us)
